TPU v7x, 512 devices: a whole 4x8x8 slice. The times are simulated.
512 devices in a mesh: clus: 64 (over z, x, core), nbr: 8 (over y).
Axes of the slice: x: 4, y: 8, z: 8, core: 2. Of those that a mesh axis runs over, the one named last changes fastest.
Arguments:
- panels: bfloat16 [2048, 16, 256], P(('clus', 'nbr')), may hold values from -6 to 6
- leaf_basis: bfloat16 [2048, 256, 64], P(('clus', 'nbr')), may hold values from -0.375 to 0.375
- transfer: bfloat16 [2048, 64, 64], P(('clus', 'nbr')), may hold values from -0.375 to 0.375
- leaf_sources: int32 [2048, 8], P(('clus', 'nbr')), may hold values from 0 to 2047, as said below
- leaf_coupling: bfloat16 [2048, 8, 64, 64], P(('clus', 'nbr')), may hold values from -0.25 to 0.25
- box_sources: int32 [512, 32], P(('clus', 'nbr')), may hold values from 0 to 511
- box_coupling: bfloat16 [512, 32, 64, 64], P(('clus', 'nbr')), may hold values from -0.125 to 0.125
- near_blocks: bfloat16 [8192, 256, 256], P(('clus', 'nbr')), may hold values from -0.125 to 0.125
- near_pairs: int32 [8192, 2], P(('clus', 'nbr')), may hold values from 0 to 2047, as said below
- near_count: int32 [512], P(('clus', 'nbr')), may hold values from 1 to 16, as said below
Outputs:
- first_product: bfloat16 [2048, 16, 256], P(('clus', 'nbr'))
- second_product: bfloat16 [2048, 16, 256], P(('clus', 'nbr'))
Inputs may be any that keep to these rules, and one draw needn't show every extreme that they name: `leaf_sources`: each entry names a leaf of the row's own group of 32 consecutive leaves. `near_pairs`: row n is a slot of device n // 16; its first leaf is not above its second, and both lie in that device's group of 32 consecutive leaves. Rows of dead slots hold such pairs too. `near_count`: some device fills all 16 slots in every draw.
All inputs are finite; a program needn't handle non-finite values.
Results may differ from a plain program's by a relative error of at most 0.013.
Values may be sent and summed in bfloat16 or wider, within the bound.
A program may use at most 64 MiB of HBM per device.

v0:
```python
import jax
import jax.numpy as jnp
from jax import lax
from jax.sharding import PartitionSpec as P


def product(
    values,
    leaf_basis,
    transfer,
    leaf_sources,
    leaf_coupling,
    box_sources,
    box_coupling,
    near_blocks,
    near_pairs,
    near_count,
):
    f32 = jnp.float32
    group_width = lax.axis_size("nbr")
    leaf_count = values.shape[0]
    group_leaves = leaf_count * group_width
    group_base = lax.axis_index("clus") * group_leaves
    leaf_coefs = jnp.einsum("trp,tpk->trk", values, leaf_basis, preferred_element_type=f32).astype(
        jnp.bfloat16
    )
    near_values = lax.all_gather(values, "nbr", axis=0, tiled=True)
    near_coefs = lax.all_gather(leaf_coefs, "nbr", axis=0, tiled=True)
    box_coefs = jnp.einsum("trk,tkm->rm", leaf_coefs, transfer, preferred_element_type=f32).astype(
        jnp.bfloat16
    )[None]
    every_box = lax.all_gather(box_coefs, ("clus", "nbr"), axis=0, tiled=True)
    chosen = jnp.take(every_box, box_sources[0], axis=0)
    box_field = jnp.einsum(
        "jrk,jkm->rm", chosen, box_coupling[0], preferred_element_type=f32
    ).astype(jnp.bfloat16)
    partner_coefs = jnp.take(near_coefs, leaf_sources - group_base, axis=0)
    leaf_field = jnp.einsum(
        "tjrk,tjkm->trm", partner_coefs, leaf_coupling, preferred_element_type=f32
    )
    descend = jnp.einsum("rm,tkm->trk", box_field, transfer, preferred_element_type=f32)
    leaf_total = (leaf_field + descend).astype(jnp.bfloat16)
    far_part = jnp.einsum("trk,tpk->trp", leaf_total, leaf_basis, preferred_element_type=f32)
    local_pairs = near_pairs - group_base
    targets = local_pairs[:, 0]
    sources = local_pairs[:, 1]
    slot_count = near_blocks.shape[0]
    live_slots = (jnp.arange(slot_count) < near_count[0]).astype(f32)
    apart_mask = live_slots * (targets != sources).astype(f32)
    from_source = jnp.einsum(
        "nrp,nqp->nrq",
        jnp.take(near_values, sources, axis=0),
        near_blocks,
        preferred_element_type=f32,
    )
    from_target = jnp.einsum(
        "nrq,nqp->nrp",
        jnp.take(near_values, targets, axis=0),
        near_blocks,
        preferred_element_type=f32,
    )
    members = jnp.arange(group_leaves)[:, None]
    onto_target = (members == targets[None, :]).astype(f32) * live_slots[None, :]
    onto_source = (members == sources[None, :]).astype(f32) * apart_mask[None, :]
    partial_value = jnp.einsum(
        "gn,nrq->grq", onto_target, from_source, precision=lax.Precision.HIGHEST
    )
    partial_value = partial_value + jnp.einsum(
        "gn,nrp->grp", onto_source, from_target, precision=lax.Precision.HIGHEST
    )
    near_part = lax.psum_scatter(partial_value, "nbr", scatter_dimension=0, tiled=True)
    return (near_part + far_part).astype(jnp.bfloat16)


def on_device(
    panels,
    leaf_basis,
    transfer,
    leaf_sources,
    leaf_coupling,
    box_sources,
    box_coupling,
    near_blocks,
    near_pairs,
    near_count,
):
    first_product = product(
        panels,
        leaf_basis,
        transfer,
        leaf_sources,
        leaf_coupling,
        box_sources,
        box_coupling,
        near_blocks,
        near_pairs,
        near_count,
    )
    second_product = product(
        first_product,
        leaf_basis,
        transfer,
        leaf_sources,
        leaf_coupling,
        box_sources,
        box_coupling,
        near_blocks,
        near_pairs,
        near_count,
    )
    return (first_product, second_product)


def solution(mesh):
    placed = (
        P(("clus", "nbr"), None, None),
        P(("clus", "nbr"), None, None),
        P(("clus", "nbr"), None, None),
        P(("clus", "nbr"), None),
        P(("clus", "nbr"), None, None, None),
        P(("clus", "nbr"), None),
        P(("clus", "nbr"), None, None, None),
        P(("clus", "nbr"), None, None),
        P(("clus", "nbr"), None),
        P(("clus", "nbr")),
    )
    return jax.shard_map(
        on_device,
        mesh=mesh,
        in_specs=placed,
        out_specs=(P(("clus", "nbr"), None, None), P(("clus", "nbr"), None, None)),
        check_vma=False,
    )
```

profile of v0, /device:TPU:1, one launch (start us, length us, event | category | flops | bytes accessed | tf_op | source)
XLA Modules:
  0.0 266.0 jit_solution(18164716219403365563)
XLA Ops:
  8.0 0.0 copy-start
  8.0 0.0 all-gather.5.cloned.1.call-start
  8.1 1.2 convolution_convert_fusion.1
  9.2 1.6 fusion.6
  10.9 0.0 all-gather.5.cloned.1.call-update
  10.9 0.0 reduce-scatter.3.cloned.1.call-start
  11.0 0.7 broadcast_subtract_fusion
  12.3 21.1 %all_gather.18 = bf16[32,16,256]{2,1,0:T(8,128)(2,1)S(1)} all-gather(bf16[4,16,256]{2,1,0:T(8,128)(2,1)} %param.16), channel_id=1, replica_groups=mesh['clus'=64,'nbr'=8] {'nbr'}, dimensions={0}, use_global_device_ids=true | all-gather | bytes 294912 | tf_op jit(solution)/shard_map/all_gather | solution.py:27
  33.4 0.6 gather_fusion.1
  34.0 0.6 gather_fusion
  34.6 0.0 copy-done
  34.6 0.7 fusion.30
  35.3 0.7 fusion.18
  36.0 0.0 copy-start.5
  36.0 0.4 fusion.28
  36.5 0.0 copy-start.6
  36.5 0.0 copy-start.1
  36.5 0.8 convolution_add_fusion.1
  37.2 0.0 copy-start.2
  37.2 0.0 copy-start.3
  37.3 1.1 copy.26
  38.4 0.0 reduce-scatter.3.cloned.1.call-update
  38.4 0.0 all-gather.7.cloned.1.call-start
  38.5 0.0 copy-done.5
  38.5 0.1 reshape.118
  38.6 19.0 %all_gather.19 = bf16[32,16,64]{2,1,0:T(8,128)(2,1)S(1)} all-gather(bf16[4,16,64]{2,1,0:T(8,128)(2,1)S(1)} %convolution_convert_fusion.1), channel_id=1, replica_groups=mesh['clus'=64,'nbr'=8] {'nbr'}, dimensions={0}, use_global_device_ids=true | all-gather | bytes 73728 | tf_op jit(solution)/shard_map/all_gather | solution.py:28
  57.6 0.6 gather_fusion.2
  58.2 0.0 copy-done.6
  58.2 0.0 copy-done.1
  58.2 0.3 convolution_bitcast_fusion.3
  58.6 76.9 %all-gather.5.cloned.1.call-done = bf16[8192,64]{1,0:T(8,128)(2,1)} async-done(((bf16[16,64]{1,0:T(8,128)(2,1)}), bf16[8192,64]{1,0:T(8,128)(2,1)}) %all-gather.5.cloned.1.call-update) | async-done | bytes 1048592 | tf_op jit(solution)/shard_map/all_gather | solution.py:32
  135.5 2.2 gather_fusion.3
  137.7 1.4 fusion.11
  139.1 0.0 reduce-scatter.3.cloned.1.call-done
  139.1 0.0 copy-done.2
  139.1 0.0 copy-done.3
  139.1 1.1 fusion
  140.3 0.0 copy-start.4
  140.3 0.1 convolution_convert_fusion
  140.4 0.8 fusion.8
  141.2 0.0 all-gather.7.cloned.1.call-update
  141.2 0.0 reduce-scatter.5.cloned.1.call-start
  141.3 18.8 %all_gather.21 = bf16[32,16,256]{2,1,0:T(8,128)(2,1)S(1)} all-gather(bf16[4,16,256]{2,1,0:T(8,128)(2,1)S(1)} %fusion), channel_id=1, replica_groups=mesh['clus'=64,'nbr'=8] {'nbr'}, dimensions={0}, use_global_device_ids=true | all-gather | bytes 294912 | tf_op jit(solution)/shard_map/all_gather | solution.py:27
  160.1 0.6 gather_fusion.5
  160.7 0.6 gather_fusion.4
  161.3 0.7 fusion.24
  161.9 0.7 fusion.15
  162.7 0.0 copy-done.4
  162.7 0.4 fusion.22
  163.1 0.8 convolution_add_fusion
  163.9 1.1 copy.29
  165.0 0.0 reduce-scatter.5.cloned.1.call-update
  165.0 18.8 %all_gather.22 = bf16[32,16,64]{2,1,0:T(8,128)(2,1)S(1)} all-gather(bf16[4,16,64]{2,1,0:T(8,128)(2,1)S(1)} %convolution_convert_fusion), channel_id=1, replica_groups=mesh['clus'=64,'nbr'=8] {'nbr'}, dimensions={0}, use_global_device_ids=true | all-gather | bytes 73728 | tf_op jit(solution)/shard_map/all_gather | solution.py:28
  183.8 0.6 gather_fusion.6
  184.4 0.3 convolution_bitcast_fusion.1
  184.7 68.5 %all-gather.7.cloned.1.call-done = bf16[8192,64]{1,0:T(8,128)(2,1)} async-done(((bf16[16,64]{1,0:T(8,128)(2,1)}), bf16[8192,64]{1,0:T(8,128)(2,1)}) %all-gather.7.cloned.1.call-update) | async-done | bytes 1048592 | tf_op jit(solution)/shard_map/all_gather | solution.py:32
  253.2 2.2 gather_fusion.7
  255.4 1.4 fusion.10
  256.8 0.0 reduce-scatter.5.cloned.1.call-done
  256.8 1.8 fusion.1
  (10 shorter events, 0.1 us)
Async XLA Ops:
  8.0 26.6 %copy-start = (bf16[16,256,256]{2,1,0:T(8,128)(2,1)S(1)}, bf16[16,256,256]{2,1,0:T(8,128)(2,1)}, u32[]{:S(2)}) copy-start(bf16[16,256,256]{2,1,0:T(8,128)(2,1)} %param.23) | copy-start | bytes 6291460
  8.0 127.5 %all-gather.5.cloned.1.call-start = ((), (), s32[]{:S(2)}) async-start(), calls=%async_computation.4 | async-start | bytes 2101248 | tf_op jit(solution)/shard_map/all_gather | solution.py:32
  10.9 128.2 %reduce-scatter.3.cloned.1.call-start = ((), (), s32[]{:S(2)}) async-start(), calls=%async_computation.2 | async-start | bytes 589824 | tf_op jit(solution)/shard_map/reduce_scatter | solution.py:71
  36.0 2.4 copy-start.5
  36.5 21.7 %copy-start.6 = (s32[1,32]{1,0:T(1,128)S(1)}, s32[1,32]{1,0:T(1,128)}, u32[]{:S(2)}) copy-start(s32[1,32]{1,0:T(1,128)} %param.21) | copy-start | bytes 388
  36.5 21.8 %copy-start.1 = (bf16[4,8,64,64]{3,2,1,0:T(8,128)(2,1)S(1)}, bf16[4,8,64,64]{3,2,1,0:T(8,128)(2,1)}, u32[]{:S(2)}) copy-start(bf16[4,8,64,64]{3,2,1,0:T(8,128)(2,1)} %param.20) | copy-start | bytes 786436
  37.2 101.9 %copy-start.2 = (bf16[4,256,64]{1,2,0:T(8,128)(2,1)S(1)}, bf16[4,256,64]{1,2,0:T(8,128)(2,1)}, u32[]{:S(2)}) copy-start(bf16[4,256,64]{1,2,0:T(8,128)(2,1)} %param.17) | copy-start | bytes 393220
  37.2 101.9 %copy-start.3 = (bf16[4,64,64]{2,1,0:T(8,128)(2,1)S(1)}, bf16[4,64,64]{2,1,0:T(8,128)(2,1)}, u32[]{:S(2)}) copy-start(bf16[4,64,64]{2,1,0:T(8,128)(2,1)} %param.18) | copy-start | bytes 98308
  38.4 214.8 %all-gather.7.cloned.1.call-start = ((), (), s32[]{:S(2)}) async-start(), calls=%async_computation.5 | async-start | bytes 2101248 | tf_op jit(solution)/shard_map/all_gather | solution.py:32
  140.3 22.4 %copy-start.4 = (bf16[4,16,256]{2,1,0:T(8,128)(2,1)}, bf16[4,16,256]{2,1,0:T(8,128)(2,1)S(1)}, u32[]{:S(2)}) copy-start(bf16[4,16,256]{2,1,0:T(8,128)(2,1)S(1)} %fusion) | copy-start | bytes 98308
  141.2 115.6 %reduce-scatter.5.cloned.1.call-start = ((), (), s32[]{:S(2)}) async-start(), calls=%async_computation.3 | async-start | bytes 589824 | tf_op jit(solution)/shard_map/reduce_scatter | solution.py:71
Sparse Core Ops, SparseCore 0:
  14.3 121.1 all-gather.4
  141.4 111.8 all-gather.6
Sparse Core Ops, SparseCore 1:
  38.5 44.1 reduce-scatter.2
  165.1 36.5 reduce-scatter.4
where the time goes:
time: 266 us
  waiting for transfers between devices  146 us (55%)
  blocking collectives  77.7 us (29%)
  between operations  16.4 us (6%)
  matrix products  15.2 us (6%)
  local copies, waits for them, and re-layouts  10.2 us (4%)
    all_gather x2, waiting for transfers between devices, product(): every_box = lax.all_gather(box_coefs, ('clus', 'nbr'), axis=0, tiled=True)  145 us
    all_gather x2, blocking collectives, product(): near_values = lax.all_gather(values, 'nbr', axis=0, tiled=True)  40 us
    all_gather x2, blocking collectives, product(): near_coefs = lax.all_gather(leaf_coefs, 'nbr', axis=0, tiled=True)  37.8 us
  transfers between devices with their start and end apart: 4, of which 2 were waited for; matrix products, arithmetic and copies ran while one was open for 7% of the time, Pallas kernels for 0%

commit v1 on v0

v1 whole, which is shorter than its diff:
```python
import jax
import jax.numpy as jnp
from jax import lax
from jax.experimental import pallas as pl
from jax.experimental.pallas import tpu as pltpu
from jax.sharding import PartitionSpec as P

MESH = pl.DeviceIdType.MESH
F32 = jnp.float32
BF16 = jnp.bfloat16
NY, NZ, NX = 8, 8, 4
LEAVES, RHS, PANELS, RANK = 4, 16, 256, 64
SLOTS, FAR_LEAF, FAR_BOX = 16, 8, 32
GROUP = NY * LEAVES
NT = (((1,), (1,)), ((), ()))
FAR_FIRST = (4, 3, 5, 2, 6, 1, 7)


def dot(a, b):
    return jnp.dot(a, b, preferred_element_type=F32)


def dot_nt(a, b):
    return lax.dot_general(a, b, NT, preferred_element_type=F32)


def iota(shape, dim):
    return lax.broadcasted_iota(jnp.int32, shape, dim)


def kernel(
    pairs, count, leaf_src, box_src,
    panels_hbm, basis_hbm, transfer_hbm, leafc_hbm, boxc_hbm, blocks_hbm,
    out0, out1,
    basis, transfer, leafc, boxw, blocks, twice, leafw, scatter, contrib,
    vals0, vals1, coefs0, coefs1, boxes0, boxes1, part0, part1, got0, got1, boxlhs, leaflhs,
    load_sem, send_sem, recv_sem,
):
    clus = lax.axis_index("clus")
    y = lax.axis_index("nbr")
    core = lax.rem(clus, 2)
    x = lax.rem(clus // 2, NX)
    z = clus // (2 * NX)

    def at(zz, xx, cc, yy):
        return ((zz * NX + xx) * 2 + cc, yy)

    def y_peer(d):
        return at(z, x, core, lax.rem(y + d, NY))

    def z_peer(d):
        return at(lax.rem(z + d, NZ), x, core, y)

    def x_peer(d):
        return at(z, lax.rem(x + d, NX), core, y)

    other = at(z, x, 1 - core, y)

    vals, coefs, boxes = (vals0, vals1), (coefs0, coefs1), (boxes0, boxes1)
    part, got, outs = (part0, part1), (got0, got1), (out0, out1)
    own_rows = pl.ds(y * LEAVES, LEAVES)

    barrier = pltpu.get_barrier_semaphore()
    greet = [y_peer(d) for d in FAR_FIRST] + [z_peer(d) for d in FAR_FIRST]
    greet += [x_peer(d) for d in (2, 1, 3)] + [other]
    for peer in greet:
        pl.semaphore_signal(barrier, inc=1, device_id=peer, device_id_type=MESH)

    loads = [
        pltpu.make_async_copy(panels_hbm, vals0.at[own_rows], load_sem.at[0]),
        pltpu.make_async_copy(basis_hbm, basis, load_sem.at[1]),
        pltpu.make_async_copy(transfer_hbm, transfer, load_sem.at[2]),
        pltpu.make_async_copy(leafc_hbm, leafc, load_sem.at[3]),
        pltpu.make_async_copy(boxc_hbm.at[0], boxw.at[:, pl.ds(0, RANK)], load_sem.at[4]),
        pltpu.make_async_copy(boxc_hbm.at[0], boxw.at[:, pl.ds(RANK, RANK)], load_sem.at[5]),
        pltpu.make_async_copy(blocks_hbm, blocks, load_sem.at[6]),
    ]
    for load in loads:
        load.start()

    lane = iota((1, 2 * RANK), 1)
    low_half = lane < RANK
    eye_row = iota((RANK, 2 * RANK), 0)
    eye_lane = iota((RANK, 2 * RANK), 1)
    loads[2].wait()
    both = (lax.rem(eye_lane, RANK) == eye_row).astype(BF16)
    twice[...] = dot(transfer[...].reshape(LEAVES * RANK, RANK), both).astype(BF16)
    loads[3].wait()
    for t in range(LEAVES):
        place = (eye_lane == eye_row + (t % 2) * RANK).astype(BF16)
        moved = dot(leafc[t].reshape(FAR_LEAF * RANK, RANK), place).astype(BF16)
        moved = moved.reshape(FAR_LEAF, RANK, 2 * RANK)
        leafw[t, :, pl.ds(0, RANK)] = moved
        leafw[t, :, pl.ds(RANK, RANK)] = moved

    slot_of = iota((1, SLOTS * RHS), 1) // RHS
    first = jnp.full((1, SLOTS * RHS), -1, jnp.int32)
    second = jnp.full((1, SLOTS * RHS), -1, jnp.int32)
    live_count = count[0]
    targets = [lax.rem(pairs[0, n], GROUP) for n in range(SLOTS)]
    sources = [lax.rem(pairs[1, n], GROUP) for n in range(SLOTS)]
    for n in range(SLOTS):
        live = n < live_count
        first = jnp.where(slot_of == n, jnp.where(live, targets[n], -1), first)
        apart = jnp.logical_and(live, targets[n] != sources[n])
        second = jnp.where(slot_of == n, jnp.where(apart, sources[n], -1), second)
    rows = NY * LEAVES * RHS
    cols = SLOTS * RHS
    row = iota((rows, cols), 0)
    same = lax.rem(row, RHS) == lax.rem(iota((rows, cols), 1), RHS)
    scatter[:, pl.ds(0, cols)] = jnp.logical_and(same, row // RHS == first).astype(BF16)
    scatter[:, pl.ds(cols, cols)] = jnp.logical_and(same, row // RHS == second).astype(BF16)

    for i in (0, 1, 4, 5, 6):
        loads[i].wait()
    pl.semaphore_wait(barrier, len(greet))

    sent = []

    class Sends:
        def __init__(self, p, base):
            self.p, self.n, self.copies = p, base, []

        def start(self, src, dst, peer):
            copy = pltpu.make_async_remote_copy(
                src_ref=src, dst_ref=dst,
                send_sem=send_sem.at[self.p, self.n], recv_sem=recv_sem.at[self.p, self.n],
                device_id=peer, device_id_type=MESH,
            )
            copy.start()
            self.n += 1
            self.copies.append(copy)
            sent.append(copy)

        def wait(self):
            for copy in self.copies:
                copy.wait_recv()

    diag_row = iota((LEAVES * RHS, LEAVES * RANK), 0) // RHS
    diag_lane = iota((LEAVES * RHS, LEAVES * RANK), 1) // RANK
    diagonal = diag_row == diag_lane

    for p in range(2):
        val, coef, box = vals[p], coefs[p], boxes[p]
        values = Sends(p, 0)
        for d in FAR_FIRST:
            values.start(val.at[own_rows], val.at[own_rows], y_peer(d))

        own = val[own_rows].reshape(LEAVES * RHS, PANELS)
        every = dot_nt(own, basis[...].reshape(LEAVES * RANK, PANELS))
        every = jnp.where(diagonal, every, 0.0).reshape(LEAVES, RHS, LEAVES * RANK)
        packed = jnp.sum(every, axis=0).astype(BF16)
        coef[y, 0] = packed[:, : 2 * RANK]
        coef[y, 1] = packed[:, 2 * RANK :]
        wide = dot(packed, twice[...])
        box[core, x, z, y] = jnp.where(low_half, wide[:8], wide[8:]).astype(BF16)
        along_y = Sends(p, 7)
        mine = box.at[core, x, z, y]
        for d in FAR_FIRST:
            along_y.start(mine, mine, y_peer(d))
        near_coefs = Sends(p, 14)
        for d in FAR_FIRST:
            near_coefs.start(coef.at[y], coef.at[y], y_peer(d))

        along_y.wait()
        along_z = Sends(p, 21)
        mine = box.at[core, x, z]
        for d in FAR_FIRST:
            along_z.start(mine, mine, z_peer(d))

        values.wait()
        for n in range(SLOTS):
            block = blocks[n]
            contrib[pl.ds(n * RHS, RHS)] = dot_nt(val[sources[n]], block).astype(BF16)
            contrib[pl.ds(cols + n * RHS, RHS)] = dot(val[targets[n]], block).astype(BF16)
        total = dot(scatter[...], contrib[...]).astype(BF16)
        part[p][...] = total.reshape(NY, LEAVES * RHS, PANELS)
        near = Sends(p, 28)
        for d in FAR_FIRST:
            near.start(part[p].at[lax.rem(y + d, NY)], got[p].at[d - 1], y_peer(d))

        along_z.wait()
        along_x = Sends(p, 35)
        mine = box.at[core, x]
        for d in (2, 1, 3):
            along_x.start(mine, mine, x_peer(d))
        across = Sends(p, 38)
        across.start(mine, mine, other)

        near_coefs.wait()
        for t in range(LEAVES):
            for j in range(FAR_LEAF):
                leaf = lax.rem(leaf_src[t, j], GROUP)
                tile = coef[lax.div(leaf, LEAVES), lax.div(lax.rem(leaf, LEAVES), 2)]
                keep = (lane // RANK) == lax.rem(leaf, 2)
                leaflhs[t, :, pl.ds(j * 2 * RANK, 2 * RANK)] = jnp.where(
                    keep, tile.astype(F32), 0.0
                ).astype(BF16)
        pair = FAR_LEAF * 2 * RANK
        fields = []
        for t in range(LEAVES):
            fields.append(dot(leaflhs[t], leafw[t].reshape(pair, 2 * RANK)))
        leaf_field = jnp.concatenate([fields[0] + fields[1], fields[2] + fields[3]], axis=1)

        for copy, d in zip(along_x.copies, (2, 1, 3)):
            copy.wait_recv()
            arrived = box.at[core, lax.rem(x + NX - d, NX)]
            across.start(arrived, arrived, other)
        across.wait()

        for j in range(FAR_BOX):
            b = box_src[0, j]
            by = lax.rem(b, NY)
            bc = lax.rem(lax.div(b, NY), 2)
            bx = lax.rem(lax.div(b, 2 * NY), NX)
            bz = lax.div(b, 2 * NY * NX)
            tile = box[bc, bx, bz, by].astype(F32)
            boxlhs[:, pl.ds(j * 2 * RANK, 2 * RANK)] = jnp.concatenate(
                [jnp.where(low_half, tile, 0.0), jnp.where(low_half, 0.0, tile)], axis=0
            ).astype(BF16)
        box_field = dot(boxlhs[...], boxw[...].reshape(FAR_BOX * 2 * RANK, RANK)).astype(BF16)
        descend = dot_nt(box_field, transfer[...].reshape(LEAVES * RANK, RANK))
        leaf_total = leaf_field + descend
        spread = jnp.where(diagonal, jnp.concatenate([leaf_total] * LEAVES, axis=0), 0.0)
        result = dot(spread.astype(BF16), basis[...].reshape(LEAVES * RANK, PANELS))

        near.wait()
        result = result + part[p][y].astype(F32)
        for d in range(1, NY):
            result = result + got[p][d - 1].astype(F32)
        result = result.astype(BF16).reshape(LEAVES, RHS, PANELS)
        outs[p][...] = result
        if p == 0:
            vals1[own_rows] = result

    for copy in sent:
        copy.wait_send()


def on_device(
    panels, leaf_basis, transfer, leaf_sources, leaf_coupling,
    box_sources, box_coupling, near_blocks, near_pairs, near_count,
):
    smem = pl.BlockSpec(memory_space=pltpu.SMEM)
    hbm = pl.BlockSpec(memory_space=pl.ANY)
    vmem = pl.BlockSpec(memory_space=pltpu.VMEM)
    product = jax.ShapeDtypeStruct((LEAVES, RHS, PANELS), BF16)
    values = pltpu.VMEM((NY * LEAVES, RHS, PANELS), BF16)
    coefs = pltpu.VMEM((NY, 2, RHS, 2 * RANK), BF16)
    boxes = pltpu.VMEM((2, NX, NZ, NY, 8, 2 * RANK), BF16)
    part = pltpu.VMEM((NY, LEAVES * RHS, PANELS), BF16)
    got = pltpu.VMEM((NY - 1, LEAVES * RHS, PANELS), BF16)
    copies = 42
    return pl.pallas_call(
        kernel,
        out_shape=(product, product),
        in_specs=[smem] * 4 + [hbm] * 6,
        out_specs=(vmem, vmem),
        scratch_shapes=[
            pltpu.VMEM((LEAVES, RANK, PANELS), BF16),
            pltpu.VMEM((LEAVES, RANK, RANK), BF16),
            pltpu.VMEM((LEAVES, FAR_LEAF, RANK, RANK), BF16),
            pltpu.VMEM((FAR_BOX, 2 * RANK, RANK), BF16),
            pltpu.VMEM((SLOTS, PANELS, PANELS), BF16),
            pltpu.VMEM((LEAVES * RANK, 2 * RANK), BF16),
            pltpu.VMEM((LEAVES, FAR_LEAF, 2 * RANK, 2 * RANK), BF16),
            pltpu.VMEM((NY * LEAVES * RHS, 2 * SLOTS * RHS), BF16),
            pltpu.VMEM((2 * SLOTS * RHS, PANELS), BF16),
            values, values, coefs, coefs, boxes, boxes, part, part, got, got,
            pltpu.VMEM((RHS, FAR_BOX * 2 * RANK), BF16),
            pltpu.VMEM((LEAVES, RHS, FAR_LEAF * 2 * RANK), BF16),
            pltpu.SemaphoreType.DMA((7,)),
            pltpu.SemaphoreType.DMA((2, copies)),
            pltpu.SemaphoreType.DMA((2, copies)),
        ],
        compiler_params=pltpu.CompilerParams(
            collective_id=0, has_side_effects=True, vmem_limit_bytes=40 << 20
        ),
        name="two_products",
    )(
        near_pairs.T, near_count, leaf_sources, box_sources,
        panels, jnp.swapaxes(leaf_basis, 1, 2), transfer, leaf_coupling,
        box_coupling, near_blocks,
    )


def solution(mesh):
    split = ("clus", "nbr")
    placed = (
        P(split, None, None),
        P(split, None, None),
        P(split, None, None),
        P(split, None),
        P(split, None, None, None),
        P(split, None),
        P(split, None, None, None),
        P(split, None, None),
        P(split, None),
        P(split),
    )
    return jax.shard_map(
        on_device,
        mesh=mesh,
        in_specs=placed,
        out_specs=(P(split, None, None), P(split, None, None)),
        check_vma=False,
    )
```

time: 266 us -> 76.1 us (0.29)
  waiting for transfers between devices: 146 us -> 0 us
  blocking collectives: 77.7 us -> 0 us
  Pallas kernels: 0 us -> 65 us
  matrix products: 15.2 us -> 0 us
  between operations: 16.4 us -> 1.31 us
    all_gather x2 -> x0, waiting for transfers between devices: 145 us -> none  [product(): every_box = lax.all_gather(box_coefs, ('clus', 'nbr'), axis=0, tiled=True)]
    all_gather x4 -> x0, blocking collectives: 77.7 us -> none  [the longest x2 40 us: product(): near_values = lax.all_gather(values, 'nbr', axis=0, tiled=True)]
    pallas_call x0 -> x1, Pallas kernels: none -> 65 us  [on_device(): pl.pallas_call(kernel, out_shape=(product, product), in_specs=[smem] * 4...]
    dot_general x18 -> x0, matrix products: 15.2 us -> none  [the longest x2 2.88 us: product(): jnp.einsum('trk,tpk->trp', leaf_total, leaf_basis, preferred_element_type...]
    unnamed x14 -> x20, local copies, waits for them, and re-layouts: 0.04 us -> 9.41 us
    gather x8 -> x0, local copies, waits for them, and re-layouts: 7.78 us -> none  [the longest x2 4.36 us: product(): chosen = jnp.take(every_box, box_sources[0], axis=0)]
  transfers between devices with their start and end apart: 4 -> 0, of which waited for: 2 -> 0; matrix products, arithmetic and copies ran while one was open for 7% -> 0% of each run, Pallas kernels for 0% -> 0%
where the time goes in v1:
time: 76.1 us; the launch traced here: 75.7 us
  Pallas kernels  65 us (85%)
  local copies, waits for them, and re-layouts  9.41 us (12%)
  between operations  1.31 us (2%)
    pallas_call x1, Pallas kernels, on_device(): pl.pallas_call(kernel, out_shape=(product, product), in_specs=[smem] * 4...  65 us
    unnamed x20, local copies, waits for them, and re-layouts  9.41 us

profile of v1, /device:TPU:1, one launch (start us, length us, event | category | flops | bytes accessed | tf_op | source)
XLA Modules:
  0.0 75.7 jit_solution(17912968537659560020)
XLA Ops:
  1.3 0.0 copy-start
  1.3 1.6 %copy-done = bf16[16,256,256]{2,1,0:T(8,128)(2,1)S(1)} copy-done((bf16[16,256,256]{2,1,0:T(8,128)(2,1)S(1)}, bf16[16,256,256]{2,1,0:T(8,128)(2,1)}, u32[]{:S(2)}) %copy-start) | copy-done | bytes 2097176
  2.9 0.0 copy-start.1
  2.9 1.0 %copy-done.1 = bf16[4,8,64,64]{3,2,1,0:T(8,128)(2,1)S(1)} copy-done((bf16[4,8,64,64]{3,2,1,0:T(8,128)(2,1)S(1)}, bf16[4,8,64,64]{3,2,1,0:T(8,128)(2,1)}, u32[]{:S(2)}) %copy-start.1) | copy-done | bytes 262168
  3.9 0.0 copy-start.2
  3.9 1.0 %copy-done.2 = bf16[1,32,64,64]{3,2,1,0:T(8,128)(2,1)S(1)} copy-done((bf16[1,32,64,64]{3,2,1,0:T(8,128)(2,1)S(1)}, bf16[1,32,64,64]{3,2,1,0:T(8,128)(2,1)}, u32[]{:S(2)}) %copy-start.2) | copy-done | bytes 262168
  5.0 0.0 copy-start.3
  5.0 0.9 %copy-done.3 = bf16[4,256,64]{1,2,0:T(8,128)(2,1)S(1)} copy-done((bf16[4,256,64]{1,2,0:T(8,128)(2,1)S(1)}, bf16[4,256,64]{1,2,0:T(8,128)(2,1)}, u32[]{:S(2)}) %copy-start.3) | copy-done | bytes 131096
  5.9 0.0 copy-start.4
  5.9 0.8 %copy-done.4 = bf16[4,64,64]{2,1,0:T(8,128)(2,1)S(1)} copy-done((bf16[4,64,64]{2,1,0:T(8,128)(2,1)S(1)}, bf16[4,64,64]{2,1,0:T(8,128)(2,1)}, u32[]{:S(2)}) %copy-start.4) | copy-done | bytes 32792
  6.7 0.0 copy-start.5
  6.7 0.8 copy-done.5
  7.5 0.0 copy-start.6
  7.5 0.7 copy-done.6
  8.1 0.0 copy-start.7
  8.1 0.7 copy-done.7
  8.8 0.0 copy-start.8
  8.8 0.7 copy-done.8
  9.5 65.0 %two_products.1 = (bf16[4,16,256]{2,1,0:T(8,128)(2,1)S(1)}, bf16[4,16,256]{2,1,0:T(8,128)(2,1)S(1)}) custom-call(s32[2,16]{1,0:T(2,128)S(1)} %bitcast.3, s32[1]{0:T(128)S(6)} %copy.14.count, s32[4,8]{1,0:T(4,128)S(1)} %copy-done.6, s32[1,32]{1,0:T(1,128)S(1)} %copy-done.8, bf16[4,16,256]{2,1,0:T(8,128)(2,1)S(1)} %copy-done.5, ...), custom_call_target="tpu_custom_call" | custom-call | tf_op jit(solution)/shard_map/two_products/pallas_call | solution.py:254
  74.5 0.6 copy.15
  75.1 0.6 copy.16
Async XLA Ops:
  1.3 1.6 %copy-start = (bf16[16,256,256]{2,1,0:T(8,128)(2,1)S(1)}, bf16[16,256,256]{2,1,0:T(8,128)(2,1)}, u32[]{:S(2)}) copy-start(bf16[16,256,256]{2,1,0:T(8,128)(2,1)} %blocks_hbm.1) | copy-start | bytes 6291460
  2.9 1.0 %copy-start.1 = (bf16[4,8,64,64]{3,2,1,0:T(8,128)(2,1)S(1)}, bf16[4,8,64,64]{3,2,1,0:T(8,128)(2,1)}, u32[]{:S(2)}) copy-start(bf16[4,8,64,64]{3,2,1,0:T(8,128)(2,1)} %leafc_hbm.1) | copy-start | bytes 786436
  3.9 1.0 %copy-start.2 = (bf16[1,32,64,64]{3,2,1,0:T(8,128)(2,1)S(1)}, bf16[1,32,64,64]{3,2,1,0:T(8,128)(2,1)}, u32[]{:S(2)}) copy-start(bf16[1,32,64,64]{3,2,1,0:T(8,128)(2,1)} %boxc_hbm.1) | copy-start | bytes 786436
  5.0 0.9 %copy-start.3 = (bf16[4,256,64]{1,2,0:T(8,128)(2,1)S(1)}, bf16[4,256,64]{1,2,0:T(8,128)(2,1)}, u32[]{:S(2)}) copy-start(bf16[4,256,64]{1,2,0:T(8,128)(2,1)} %param.11) | copy-start | bytes 393220
  5.9 0.8 %copy-start.4 = (bf16[4,64,64]{2,1,0:T(8,128)(2,1)S(1)}, bf16[4,64,64]{2,1,0:T(8,128)(2,1)}, u32[]{:S(2)}) copy-start(bf16[4,64,64]{2,1,0:T(8,128)(2,1)} %transfer_hbm.1) | copy-start | bytes 98308
  6.7 0.8 %copy-start.5 = (bf16[4,16,256]{2,1,0:T(8,128)(2,1)S(1)}, bf16[4,16,256]{2,1,0:T(8,128)(2,1)}, u32[]{:S(2)}) copy-start(bf16[4,16,256]{2,1,0:T(8,128)(2,1)} %panels_hbm.1) | copy-start | bytes 98308
  7.5 0.7 copy-start.6
  8.1 0.7 copy-start.7
  8.8 0.7 copy-start.8

commit v2 on v1

v2 whole, which is shorter than its diff:
```python
import jax
import jax.numpy as jnp
from jax import lax
from jax.experimental import pallas as pl
from jax.experimental.pallas import tpu as pltpu
from jax.sharding import PartitionSpec as P

MESH = pl.DeviceIdType.MESH
F32 = jnp.float32
BF16 = jnp.bfloat16
NY, NZ, NX = 8, 8, 4
LEAVES, RHS, PANELS, RANK = 4, 16, 256, 64
HALF = RHS // 2
WIDE = LEAVES * RANK
SLOTS, FAR_LEAF, FAR_BOX = 16, 8, 32
GROUP = NY * LEAVES
NT = (((1,), (1,)), ((), ()))
FAR_FIRST = (4, 3, 5, 2, 6, 1, 7)
ORDER = {0: 0, 1: 1, 7: 2, 2: 3, 6: 4, 3: 5, 5: 6, 4: 7}
NEAR, ALL = 5, 8


def dot(a, b):
    return jnp.dot(a, b, preferred_element_type=F32)


def dot_nt(a, b):
    return lax.dot_general(a, b, NT, preferred_element_type=F32)


def iota(shape, dim):
    return lax.broadcasted_iota(jnp.int32, shape, dim)


def ring_slot(distance):
    return jnp.where(distance > 4, 2 * (8 - distance), jnp.maximum(2 * distance - 1, 0))


def kernel(
    pairs, count, leaf_src, box_src, box_src_hbm,
    panels_hbm, basis_hbm, transfer_hbm, leafc_hbm, boxc_hbm, blocks_hbm,
    out_hbm,
    basis, transfer, leafc, boxw, blocks, twice, leafw, scatter, contrib,
    vals00, vals01, vals10, vals11, coefs0, coefs1, boxes0, boxes1, part0, part1, got0, got1,
    last, boxlhs, leaflhs, give0, give1, take0, take1, other_src, other_src_smem,
    load_sem, store_sem, send_sem, recv_sem,
):
    clus = lax.axis_index("clus")
    y = lax.axis_index("nbr")
    core = lax.rem(clus, 2)
    x = lax.rem(lax.div(clus, 2), NX)
    z = lax.div(clus, 2 * NX)

    def at(zz, xx, cc, yy):
        return ((zz * NX + xx) * 2 + cc, yy)

    def y_peer(d):
        return at(z, x, core, lax.rem(y + d, NY))

    def z_peer(d):
        return at(lax.rem(z + d, NZ), x, core, y)

    def x_peer(d):
        return at(z, lax.rem(x + d, NX), core, y)

    other = at(z, x, 1 - core, y)
    own = pl.ds(y * LEAVES, LEAVES)

    barrier = pltpu.get_barrier_semaphore()
    greet = [y_peer(d) for d in FAR_FIRST] + [z_peer(d) for d in FAR_FIRST]
    greet += [x_peer(d) for d in (2, 1, 3)] + [other]
    for peer in greet:
        pl.semaphore_signal(barrier, inc=1, device_id=peer, device_id_type=MESH)

    def load(i, src, dst):
        copy = pltpu.make_async_copy(src, dst, load_sem.at[i])
        copy.start()
        return copy

    loads = [
        load(0, panels_hbm.at[:, pl.ds(0, HALF)], vals00.at[own]),
        load(1, panels_hbm.at[:, pl.ds(HALF, HALF)], vals01.at[own]),
        load(2, basis_hbm, basis),
        load(3, transfer_hbm, transfer),
        load(4, leafc_hbm, leafc),
        load(5, boxc_hbm.at[0], boxw.at[0, :, pl.ds(0, RANK)]),
        load(6, boxc_hbm.at[0], boxw.at[0, :, pl.ds(RANK, RANK)]),
        load(7, blocks_hbm, blocks),
    ]

    lane = iota((1, 2 * RANK), 1)
    low_half = lane < RANK
    eye_row = iota((RANK, 2 * RANK), 0)
    eye_lane = iota((RANK, 2 * RANK), 1)
    diag_row = jnp.bitwise_and(lax.shift_right_logical(iota((LEAVES * RHS, WIDE), 0), 3), LEAVES - 1)
    diagonal = diag_row == lax.shift_right_logical(iota((LEAVES * RHS, WIDE), 1), 6)

    loads[3].wait()
    both = (jnp.bitwise_and(eye_lane, RANK - 1) == eye_row).astype(BF16)
    twice[...] = dot(transfer[...].reshape(WIDE, RANK), both).astype(BF16)

    def upward(val, coef, box):
        mine = jnp.concatenate(
            [val[h][own].reshape(LEAVES * HALF, PANELS) for h in range(2)], axis=0
        )
        every = dot_nt(mine, basis[...].reshape(WIDE, PANELS))
        every = jnp.where(diagonal, every, 0.0).reshape(2, LEAVES, HALF, WIDE)
        packed = jnp.sum(every, axis=1).reshape(RHS, WIDE).astype(BF16)
        coef[y, 0] = packed[:, : 2 * RANK]
        coef[y, 1] = packed[:, 2 * RANK :]
        wide = dot(packed, twice[...])
        box[0, 0] = jnp.where(low_half, wide[:HALF], wide[HALF:]).astype(BF16)

    targets = [lax.rem(pairs[0, n], GROUP) for n in range(SLOTS)]
    sources = [lax.rem(pairs[1, n], GROUP) for n in range(SLOTS)]

    def prepare():
        side = iota((1, 2 * SLOTS * HALF), 1)
        slot = lax.shift_right_logical(side, 3)
        onto = jnp.full(side.shape, -1, jnp.int32)
        live_count = count[0]
        for n in range(SLOTS):
            live = n < live_count
            onto = jnp.where(slot == n, jnp.where(live, targets[n], -1), onto)
            apart = jnp.logical_and(live, targets[n] != sources[n])
            onto = jnp.where(slot == n + SLOTS, jnp.where(apart, sources[n], -1), onto)
        square = (GROUP * HALF, 2 * SLOTS * HALF)
        row = iota(square, 0)
        same = jnp.bitwise_and(row, HALF - 1) == jnp.bitwise_and(iota(square, 1), HALF - 1)
        hit = jnp.logical_and(same, lax.shift_right_logical(row, 3) == onto)
        scatter[...] = hit.astype(BF16)
        loads[4].wait()
        for t in range(LEAVES):
            place = (eye_lane == eye_row + (t % 2) * RANK).astype(BF16)
            moved = dot(leafc[t].reshape(FAR_LEAF * RANK, RANK), place).astype(BF16)
            moved = moved.reshape(FAR_LEAF, RANK, 2 * RANK)
            leafw[t, :, pl.ds(0, RANK)] = moved
            leafw[t, :, pl.ds(RANK, RANK)] = moved

    for i in (0, 1, 2):
        loads[i].wait()
    upward((vals00, vals01), coefs0, boxes0)
    pl.semaphore_wait(barrier, len(greet))

    pending = []

    class Sends:
        def __init__(self, p, k, whole):
            self.p, self.k = p, k
            pending.append((whole, send_sem.at[p, k]))

        def start(self, src, dst, peer, arrival=None):
            pltpu.make_async_remote_copy(
                src_ref=src, dst_ref=dst,
                send_sem=send_sem.at[self.p, self.k],
                recv_sem=recv_sem.at[self.p, self.k if arrival is None else arrival],
                device_id=peer, device_id_type=MESH,
            ).start()

    def finish(p, k, whole):
        pltpu.make_async_copy(whole, whole, recv_sem.at[p, k]).wait()

    V0, V1, C, YN, YF, ZN, ZF, X0, X1, K, R0, R1, W, S = range(14)

    for p in range(2):
        val, coef, box = (
            ((vals00, vals01), coefs0, boxes0),
            ((vals10, vals11), coefs1, boxes1),
        )[p]
        part, got = ((part0, got0), (part1, got1))[p]
        give, take = ((give0, take0), (give1, take1))[p]

        def send_values(h):
            group = Sends(p, (V0, V1)[h], val[h].at[pl.ds(0, 7 * LEAVES)])
            for d in FAR_FIRST:
                group.start(val[h].at[own], val[h].at[own], y_peer(d))

        def near_half(h):
            finish(p, (V0, V1)[h], val[h].at[pl.ds(0, 7 * LEAVES)])
            for n in range(0, SLOTS, 2):
                ahead = [dot_nt(val[h][sources[n + i]], blocks[n + i]) for i in range(2)]
                back = [dot(val[h][targets[n + i]], blocks[n + i]) for i in range(2)]
                contrib[h, pl.ds(n * HALF, RHS)] = jnp.concatenate(ahead, 0).astype(BF16)
                contrib[h, pl.ds((SLOTS + n) * HALF, RHS)] = jnp.concatenate(back, 0).astype(BF16)
            total = dot(scatter[...], contrib[h]).astype(BF16)
            part[h] = total.reshape(NY, LEAVES * HALF, PANELS)
            group = Sends(p, (R0, R1)[h], got.at[h])
            for d in FAR_FIRST:
                group.start(part.at[h, lax.rem(y + d, NY)], got.at[h, d - 1], y_peer(d))

        if p == 1:
            upward(val, coef, box)
        group = Sends(p, YN, box.at[0, pl.ds(1, 7)])
        for d in FAR_FIRST:
            slot = ORDER[8 - d]
            group.start(box.at[0, 0], box.at[0, slot], y_peer(d), YN if slot < NEAR else YF)
        send_values(0)
        send_values(1)
        if p == 0:
            Sends(0, S, other_src).start(box_src_hbm, other_src, other)
        group = Sends(p, C, coef.at[pl.ds(0, 7)])
        for d in FAR_FIRST:
            group.start(coef.at[y], coef.at[y], y_peer(d))

        if p == 0:
            prepare()
            for i in (5, 6, 7):
                loads[i].wait()
            Sends(0, W, boxw.at[1]).start(boxw.at[0], boxw.at[1], other)
            finish(0, S, other_src)
            to_smem = pltpu.make_async_copy(other_src, other_src_smem, load_sem.at[8])
            to_smem.start()
            to_smem.wait()

        for k, a, b in ((YN, 0, NEAR), (YF, NEAR, ALL)):
            finish(p, k, box.at[0, pl.ds(max(a, 1), b - max(a, 1))])
            group = Sends(p, (ZN, ZF)[a > 0], box.at[0, pl.ds(0, 7 * (b - a))])
            for d in FAR_FIRST:
                slot = ORDER[8 - d]
                group.start(
                    box.at[0, pl.ds(a, b - a)], box.at[0, pl.ds(8 * slot + a, b - a)],
                    z_peer(d), ZN if slot < NEAR else ZF,
                )

        def send_x(a, b, k):
            group = Sends(p, k, box.at[pl.ds(1, 3), pl.ds(8 * a, 8 * (b - a))])
            rows = pl.ds(8 * a, 8 * (b - a))
            for d in (2, 1, 3):
                group.start(box.at[0, rows], box.at[NX - d, rows], x_peer(d))

        near_half(0)
        finish(p, ZN, box.at[0, pl.ds(8, 8 * (NEAR - 1))])
        send_x(0, NEAR, X0)
        near_half(1)
        finish(p, ZF, box.at[0, pl.ds(8 * NEAR, 8 * (ALL - NEAR))])
        send_x(NEAR, ALL, X1)

        finish(p, C, coef.at[pl.ds(0, 7)])
        for t in range(LEAVES):
            for j in range(FAR_LEAF):
                leaf = lax.rem(leaf_src[t, j], GROUP)
                tile = coef[lax.div(leaf, LEAVES), lax.div(lax.rem(leaf, LEAVES), 2)]
                keep = lax.shift_right_logical(lane, 6) == lax.rem(leaf, 2)
                leaflhs[t, :, pl.ds(j * 2 * RANK, 2 * RANK)] = jnp.where(
                    keep, tile.astype(F32), 0.0
                ).astype(BF16)
        pair = FAR_LEAF * 2 * RANK
        fields = []
        for t in range(LEAVES):
            fields.append(dot(leaflhs[t], leafw[t].reshape(pair, 2 * RANK)))
        leaf_field = jnp.concatenate([fields[0] + fields[1], fields[2] + fields[3]], axis=1)

        for a, b, k in ((0, NEAR, X0), (NEAR, ALL, X1)):
            finish(p, k, box.at[pl.ds(1, 3), pl.ds(8 * a, 8 * (b - a))])
        if p == 0:
            finish(0, W, boxw.at[1])

        def box_part(g):
            src = (box_src, other_src_smem)[g]
            for j in range(FAR_BOX):
                b = src[0, j]
                by = lax.rem(lax.rem(b, NY) + NY - y, NY)
                held = lax.rem(lax.div(b, NY), 2) == core
                bx = lax.rem(lax.rem(lax.div(b, 2 * NY), NX) + NX - x, NX)
                bz = lax.rem(lax.rem(lax.div(b, 2 * NY * NX), NZ) + NZ - z, NZ)
                tile = box[bx, ring_slot(bz) * NY + ring_slot(by)].astype(F32)
                tile = jnp.where(held, tile, 0.0)
                boxlhs[g, :, pl.ds(j * 2 * RANK, 2 * RANK)] = jnp.concatenate(
                    [jnp.where(low_half, tile, 0.0), jnp.where(low_half, 0.0, tile)], axis=0
                ).astype(BF16)
            return dot(boxlhs[g], boxw[g].reshape(FAR_BOX * 2 * RANK, RANK))

        give[...] = box_part(1)
        Sends(p, K, take).start(give, take, other)
        box_field = box_part(0)
        finish(p, K, take)
        box_field = (box_field + take[...]).astype(BF16)
        descend = dot_nt(box_field, transfer[...].reshape(WIDE, RANK))
        leaf_total = leaf_field + descend
        spread = jnp.concatenate(
            [leaf_total[:HALF]] * LEAVES + [leaf_total[HALF:]] * LEAVES, axis=0
        )
        spread = jnp.where(diagonal, spread, 0.0).astype(BF16)
        far = dot(spread, basis[...].reshape(WIDE, PANELS))

        result = []
        for h in range(2):
            finish(p, (R0, R1)[h], got.at[h])
            near = part[h, y].astype(F32)
            for d in range(1, NY):
                near = near + got[h, d - 1].astype(F32)
            near = near + far[h * LEAVES * HALF : (h + 1) * LEAVES * HALF]
            near = near.astype(BF16).reshape(LEAVES, HALF, PANELS)
            if p == 0:
                (vals10, vals11)[h][own] = near
            else:
                last[h] = near
        for h in range(2):
            pltpu.make_async_copy(
                (vals10, vals11)[h].at[own] if p == 0 else last.at[h],
                out_hbm.at[p, :, pl.ds(h * HALF, HALF)],
                store_sem.at[p, h],
            ).start()

    for whole, sem in pending:
        pltpu.make_async_copy(whole, whole, sem).wait()
    for p in range(2):
        for h in range(2):
            pltpu.make_async_copy(
                (vals10, vals11)[h].at[own] if p == 0 else last.at[h],
                out_hbm.at[p, :, pl.ds(h * HALF, HALF)],
                store_sem.at[p, h],
            ).wait()


def on_device(
    panels, leaf_basis, transfer, leaf_sources, leaf_coupling,
    box_sources, box_coupling, near_blocks, near_pairs, near_count,
):
    smem = pl.BlockSpec(memory_space=pltpu.SMEM)
    hbm = pl.BlockSpec(memory_space=pl.ANY)
    products = jax.ShapeDtypeStruct((2, LEAVES, RHS, PANELS), BF16)
    values = pltpu.VMEM((GROUP, HALF, PANELS), BF16)
    coefs = pltpu.VMEM((NY, 2, RHS, 2 * RANK), BF16)
    boxes = pltpu.VMEM((NX, NZ * NY, HALF, 2 * RANK), BF16)
    part = pltpu.VMEM((2, NY, LEAVES * HALF, PANELS), BF16)
    got = pltpu.VMEM((2, NY - 1, LEAVES * HALF, PANELS), BF16)
    field = pltpu.VMEM((RHS, RANK), F32)
    both = pl.pallas_call(
        kernel,
        out_shape=products,
        in_specs=[smem] * 4 + [hbm] * 7,
        out_specs=hbm,
        scratch_shapes=[
            pltpu.VMEM((LEAVES, RANK, PANELS), BF16),
            pltpu.VMEM((LEAVES, RANK, RANK), BF16),
            pltpu.VMEM((LEAVES, FAR_LEAF, RANK, RANK), BF16),
            pltpu.VMEM((2, FAR_BOX, 2 * RANK, RANK), BF16),
            pltpu.VMEM((SLOTS, PANELS, PANELS), BF16),
            pltpu.VMEM((WIDE, 2 * RANK), BF16),
            pltpu.VMEM((LEAVES, FAR_LEAF, 2 * RANK, 2 * RANK), BF16),
            pltpu.VMEM((GROUP * HALF, 2 * SLOTS * HALF), BF16),
            pltpu.VMEM((2, 2 * SLOTS * HALF, PANELS), BF16),
            values, values, values, values, coefs, coefs, boxes, boxes, part, part, got, got,
            pltpu.VMEM((2, LEAVES, HALF, PANELS), BF16),
            pltpu.VMEM((2, RHS, FAR_BOX * 2 * RANK), BF16),
            pltpu.VMEM((LEAVES, RHS, FAR_LEAF * 2 * RANK), BF16),
            field, field, field, field,
            pltpu.VMEM((1, FAR_BOX), jnp.int32),
            pltpu.SMEM((1, FAR_BOX), jnp.int32),
            pltpu.SemaphoreType.DMA((9,)),
            pltpu.SemaphoreType.DMA((2, 2)),
            pltpu.SemaphoreType.DMA((2, 14)),
            pltpu.SemaphoreType.DMA((2, 14)),
        ],
        compiler_params=pltpu.CompilerParams(
            collective_id=0, has_side_effects=True, vmem_limit_bytes=63 << 20
        ),
        name="two_products",
    )(
        near_pairs.T, near_count, leaf_sources, box_sources, box_sources,
        panels, jnp.swapaxes(leaf_basis, 1, 2), transfer, leaf_coupling,
        box_coupling, near_blocks,
    )
    return both[0], both[1]


def solution(mesh):
    split = ("clus", "nbr")
    placed = (
        P(split, None, None),
        P(split, None, None),
        P(split, None, None),
        P(split, None),
        P(split, None, None, None),
        P(split, None),
        P(split, None, None, None),
        P(split, None, None),
        P(split, None),
        P(split),
    )
    return jax.shard_map(
        on_device,
        mesh=mesh,
        in_specs=placed,
        out_specs=(P(split, None, None), P(split, None, None)),
        check_vma=False,
    )
```

time: 76.1 us -> 55.8 us (0.73)
  Pallas kernels: 65 us -> 52.9 us
  local copies, waits for them, and re-layouts: 9.41 us -> 1.4 us
    pallas_call x1, Pallas kernels: 65 us -> 52.9 us  [on_device(): pl.pallas_call(kernel, out_shape=products, in_specs=[smem] * 4 + [hbm] *...]
    unnamed x20 -> x0, local copies, waits for them, and re-layouts: 9.41 us -> none
    squeeze x0 -> x1, local copies, waits for them, and re-layouts: none -> 1.4 us  [on_device(): return (both[0], both[1])]
where the time goes in v2:
time: 55.8 us; the launch traced here: 55.6 us
  Pallas kernels  52.9 us (95%)
  local copies, waits for them, and re-layouts  1.4 us (3%)
  between operations  1.29 us (2%)
    pallas_call x1, Pallas kernels, on_device(): pl.pallas_call(kernel, out_shape=products, in_specs=[smem] * 4 + [hbm] *...  52.9 us
    squeeze x1, local copies, waits for them, and re-layouts, on_device(): return (both[0], both[1])  1.4 us

profile of v2, /device:TPU:1, one launch (start us, length us, event | category | flops | bytes accessed | tf_op | source)
XLA Modules:
  0.0 55.6 jit_solution(6160718635977282851)
XLA Ops:
  1.3 52.9 %two_products.1 = bf16[2,4,16,256]{3,2,1,0:T(8,128)(2,1)} custom-call(s32[2,16]{1,0:T(2,128)} %bitcast.7, s32[1]{0:T(128)S(6)} %copy.12.count, s32[4,8]{1,0:T(4,128)} %leaf_src.1, s32[1,32]{1,0:T(1,128)} %box_src_hbm.1, s32[1,32]{1,0:T(1,128)} %box_src_hbm.1, bf16[4,16,256]{2,1,0:T(8,128)(2,1)} %panels_hbm.1, bf16[4,64,256]{2,1,0:T(8,128)(2,1)} %bitcast.6, ...), custom_call_target="tpu_custom_call" | custom-call | tf_op jit(solution)/shard_map/two_products/pallas_call | solution.py:329
  54.2 1.4 %slice_bitcast_fusion = (bf16[4,16,256]{2,1,0:T(8,128)(2,1)}, bf16[4,16,256]{2,1,0:T(8,128)(2,1)}) fusion(bf16[2,4,16,256]{3,2,1,0:T(8,128)(2,1)} %two_products.1), kind=kLoop, calls=%fused_computation | loop fusion | bytes 131072 | tf_op jit(solution)/shard_map/squeeze | solution.py:365

commit v3 on v2

--- a/solution.py
+++ b/solution.py
@@ -14,8 +14,11 @@
 WIDE = LEAVES * RANK
 SLOTS, FAR_LEAF, FAR_BOX = 16, 8, 32
 GROUP = NY * LEAVES
+PLANE = NZ * NY
+BOXES = NX * PLANE
 NT = (((1,), (1,)), ((), ()))
 FAR_FIRST = (4, 3, 5, 2, 6, 1, 7)
+NEAR_FIRST = FAR_FIRST[::-1]
 ORDER = {0: 0, 1: 1, 7: 2, 2: 3, 6: 4, 3: 5, 5: 6, 4: 7}
 NEAR, ALL = 5, 8
 
@@ -37,13 +40,13 @@
 
 
 def kernel(
-    pairs, count, leaf_src, box_src, box_src_hbm,
+    pairs_hbm, count_hbm, leaf_src_hbm, box_src_hbm,
     panels_hbm, basis_hbm, transfer_hbm, leafc_hbm, boxc_hbm, blocks_hbm,
     out_hbm,
     basis, transfer, leafc, boxw, blocks, twice, leafw, scatter, contrib,
     vals00, vals01, vals10, vals11, coefs0, coefs1, boxes0, boxes1, part0, part1, got0, got1,
     last, boxlhs, leaflhs, give0, give1, take0, take1, other_src, other_src_smem,
-    load_sem, store_sem, send_sem, recv_sem,
+    pairs, count, leaf_src, box_src, where, down, load_sem, store_sem, send_sem, recv_sem,
 ):
     clus = lax.axis_index("clus")
     y = lax.axis_index("nbr")
@@ -65,12 +68,6 @@
 
     other = at(z, x, 1 - core, y)
     own = pl.ds(y * LEAVES, LEAVES)
-
-    barrier = pltpu.get_barrier_semaphore()
-    greet = [y_peer(d) for d in FAR_FIRST] + [z_peer(d) for d in FAR_FIRST]
-    greet += [x_peer(d) for d in (2, 1, 3)] + [other]
-    for peer in greet:
-        pl.semaphore_signal(barrier, inc=1, device_id=peer, device_id_type=MESH)
 
     def load(i, src, dst):
         copy = pltpu.make_async_copy(src, dst, load_sem.at[i])
@@ -86,7 +83,17 @@
         load(5, boxc_hbm.at[0], boxw.at[0, :, pl.ds(0, RANK)]),
         load(6, boxc_hbm.at[0], boxw.at[0, :, pl.ds(RANK, RANK)]),
         load(7, blocks_hbm, blocks),
+        load(9, pairs_hbm, pairs),
+        load(10, count_hbm, count),
+        load(11, leaf_src_hbm, leaf_src),
+        load(12, box_src_hbm, box_src),
     ]
+
+    barrier = pltpu.get_barrier_semaphore()
+    greet = [y_peer(d) for d in FAR_FIRST] + [z_peer(d) for d in FAR_FIRST]
+    greet += [x_peer(d) for d in (2, 1, 3)] + [other]
+    for peer in greet:
+        pl.semaphore_signal(barrier, inc=1, device_id=peer, device_id_type=MESH)
 
     lane = iota((1, 2 * RANK), 1)
     low_half = lane < RANK
@@ -109,10 +116,8 @@
         coef[y, 0] = packed[:, : 2 * RANK]
         coef[y, 1] = packed[:, 2 * RANK :]
         wide = dot(packed, twice[...])
-        box[0, 0] = jnp.where(low_half, wide[:HALF], wide[HALF:]).astype(BF16)
-
-    targets = [lax.rem(pairs[0, n], GROUP) for n in range(SLOTS)]
-    sources = [lax.rem(pairs[1, n], GROUP) for n in range(SLOTS)]
+        box[0] = jnp.where(low_half, wide[:HALF], wide[HALF:]).astype(BF16)
+        box[BOXES] = jnp.zeros((HALF, 2 * RANK), BF16)
 
     def prepare():
         side = iota((1, 2 * SLOTS * HALF), 1)
@@ -129,6 +134,10 @@
         same = jnp.bitwise_and(row, HALF - 1) == jnp.bitwise_and(iota(square, 1), HALF - 1)
         hit = jnp.logical_and(same, lax.shift_right_logical(row, 3) == onto)
         scatter[...] = hit.astype(BF16)
+        for t in range(LEAVES):
+            down[:, pl.ds(t * PANELS, PANELS)] = lax.dot_general(
+                transfer[t], basis[t], (((0,), (0,)), ((), ())), preferred_element_type=F32
+            ).astype(BF16)
         loads[4].wait()
         for t in range(LEAVES):
             place = (eye_lane == eye_row + (t % 2) * RANK).astype(BF16)
@@ -141,6 +150,11 @@
         loads[i].wait()
     upward((vals00, vals01), coefs0, boxes0)
     pl.semaphore_wait(barrier, len(greet))
+    for i in (8, 9, 10, 11):
+        loads[i].wait()
+    targets = [lax.rem(pairs[0, n], GROUP) for n in range(SLOTS)]
+    sources = [lax.rem(pairs[1, n], GROUP) for n in range(SLOTS)]
+
 
     pending = []
 
@@ -160,7 +174,9 @@
     def finish(p, k, whole):
         pltpu.make_async_copy(whole, whole, recv_sem.at[p, k]).wait()
 
-    V0, V1, C, YN, YF, ZN, ZF, X0, X1, K, R0, R1, W, S = range(14)
+    V0, V1, C, YN, YF, Z1, Z2, Z3, Z4, X, K, R0, R1, W, S = range(15)
+    z_chunks = ((Z1, 1, 3), (Z2, 3, 5), (Z3, 5, 7), (Z4, 7, 8))
+    z_sem = {slot: k for k, a, b in z_chunks for slot in range(a, b)}
 
     for p in range(2):
         val, coef, box = (
@@ -190,10 +206,10 @@
 
         if p == 1:
             upward(val, coef, box)
-        group = Sends(p, YN, box.at[0, pl.ds(1, 7)])
+        along_y = Sends(p, YN, box.at[pl.ds(1, 7)])
         for d in FAR_FIRST:
             slot = ORDER[8 - d]
-            group.start(box.at[0, 0], box.at[0, slot], y_peer(d), YN if slot < NEAR else YF)
+            along_y.start(box.at[0], box.at[slot], y_peer(d), YN if slot < NEAR else YF)
         send_values(0)
         send_values(1)
         if p == 0:
@@ -211,29 +227,46 @@
             to_smem = pltpu.make_async_copy(other_src, other_src_smem, load_sem.at[8])
             to_smem.start()
             to_smem.wait()
+            for g, src in enumerate((box_src, other_src_smem)):
+                for j in range(FAR_BOX):
+                    b = src[0, j]
+                    by = lax.rem(lax.rem(b, NY) + NY - y, NY)
+                    bx = lax.rem(lax.rem(lax.div(b, 2 * NY), NX) + NX - x, NX)
+                    bz = lax.rem(lax.rem(lax.div(b, 2 * NY * NX), NZ) + NZ - z, NZ)
+                    spot = bx * PLANE + ring_slot(bz) * NY + ring_slot(by)
+                    held = lax.rem(lax.div(b, NY), 2) == core
+                    where[g, j] = jnp.where(held, spot, BOXES)
 
         for k, a, b in ((YN, 0, NEAR), (YF, NEAR, ALL)):
-            finish(p, k, box.at[0, pl.ds(max(a, 1), b - max(a, 1))])
-            group = Sends(p, (ZN, ZF)[a > 0], box.at[0, pl.ds(0, 7 * (b - a))])
-            for d in FAR_FIRST:
+            finish(p, k, box.at[pl.ds(max(a, 1), b - max(a, 1))])
+            along_z = Sends(p, (Z1, Z2)[a > 0], box.at[pl.ds(0, 7 * (b - a))])
+            for d in NEAR_FIRST:
                 slot = ORDER[8 - d]
-                group.start(
-                    box.at[0, pl.ds(a, b - a)], box.at[0, pl.ds(8 * slot + a, b - a)],
-                    z_peer(d), ZN if slot < NEAR else ZF,
+                along_z.start(
+                    box.at[pl.ds(a, b - a)], box.at[pl.ds(8 * slot + a, b - a)],
+                    z_peer(d), z_sem[slot],
                 )
 
-        def send_x(a, b, k):
-            group = Sends(p, k, box.at[pl.ds(1, 3), pl.ds(8 * a, 8 * (b - a))])
-            rows = pl.ds(8 * a, 8 * (b - a))
+        along_x = Sends(p, X, box.at[pl.ds(PLANE, 3 * PLANE)])
+
+        def send_x(a, b):
             for d in (2, 1, 3):
-                group.start(box.at[0, rows], box.at[NX - d, rows], x_peer(d))
-
+                along_x.start(
+                    box.at[pl.ds(8 * a, 8 * (b - a))],
+                    box.at[pl.ds((NX - d) * PLANE + 8 * a, 8 * (b - a))],
+                    x_peer(d),
+                )
+
+        def forward(chunk):
+            k, a, b = z_chunks[chunk]
+            finish(p, k, box.at[pl.ds(8 * a, 8 * (b - a))])
+            send_x(a, b)
+
+        send_x(0, 1)
         near_half(0)
-        finish(p, ZN, box.at[0, pl.ds(8, 8 * (NEAR - 1))])
-        send_x(0, NEAR, X0)
+        for chunk in range(4):
+            forward(chunk)
         near_half(1)
-        finish(p, ZF, box.at[0, pl.ds(8 * NEAR, 8 * (ALL - NEAR))])
-        send_x(NEAR, ALL, X1)
 
         finish(p, C, coef.at[pl.ds(0, 7)])
         for t in range(LEAVES):
@@ -250,21 +283,19 @@
             fields.append(dot(leaflhs[t], leafw[t].reshape(pair, 2 * RANK)))
         leaf_field = jnp.concatenate([fields[0] + fields[1], fields[2] + fields[3]], axis=1)
 
-        for a, b, k in ((0, NEAR, X0), (NEAR, ALL, X1)):
-            finish(p, k, box.at[pl.ds(1, 3), pl.ds(8 * a, 8 * (b - a))])
+        spread = jnp.concatenate(
+            [leaf_field[:HALF]] * LEAVES + [leaf_field[HALF:]] * LEAVES, axis=0
+        )
+        spread = jnp.where(diagonal, spread, 0.0).astype(BF16)
+        from_leaves = dot(spread, basis[...].reshape(WIDE, PANELS))
+
+        finish(p, X, box.at[pl.ds(PLANE, 3 * PLANE)])
         if p == 0:
             finish(0, W, boxw.at[1])
 
         def box_part(g):
-            src = (box_src, other_src_smem)[g]
             for j in range(FAR_BOX):
-                b = src[0, j]
-                by = lax.rem(lax.rem(b, NY) + NY - y, NY)
-                held = lax.rem(lax.div(b, NY), 2) == core
-                bx = lax.rem(lax.rem(lax.div(b, 2 * NY), NX) + NX - x, NX)
-                bz = lax.rem(lax.rem(lax.div(b, 2 * NY * NX), NZ) + NZ - z, NZ)
-                tile = box[bx, ring_slot(bz) * NY + ring_slot(by)].astype(F32)
-                tile = jnp.where(held, tile, 0.0)
+                tile = box[where[g, j]].astype(F32)
                 boxlhs[g, :, pl.ds(j * 2 * RANK, 2 * RANK)] = jnp.concatenate(
                     [jnp.where(low_half, tile, 0.0), jnp.where(low_half, 0.0, tile)], axis=0
                 ).astype(BF16)
@@ -275,13 +306,7 @@
         box_field = box_part(0)
         finish(p, K, take)
         box_field = (box_field + take[...]).astype(BF16)
-        descend = dot_nt(box_field, transfer[...].reshape(WIDE, RANK))
-        leaf_total = leaf_field + descend
-        spread = jnp.concatenate(
-            [leaf_total[:HALF]] * LEAVES + [leaf_total[HALF:]] * LEAVES, axis=0
-        )
-        spread = jnp.where(diagonal, spread, 0.0).astype(BF16)
-        far = dot(spread, basis[...].reshape(WIDE, PANELS))
+        from_box = dot(box_field, down[...])
 
         result = []
         for h in range(2):
@@ -289,7 +314,14 @@
             near = part[h, y].astype(F32)
             for d in range(1, NY):
                 near = near + got[h, d - 1].astype(F32)
-            near = near + far[h * LEAVES * HALF : (h + 1) * LEAVES * HALF]
+            near = near + from_leaves[h * LEAVES * HALF : (h + 1) * LEAVES * HALF]
+            near = near + jnp.concatenate(
+                [
+                    from_box[h * HALF : (h + 1) * HALF, t * PANELS : (t + 1) * PANELS]
+                    for t in range(LEAVES)
+                ],
+                axis=0,
+            )
             near = near.astype(BF16).reshape(LEAVES, HALF, PANELS)
             if p == 0:
                 (vals10, vals11)[h][own] = near
@@ -317,19 +349,18 @@
     panels, leaf_basis, transfer, leaf_sources, leaf_coupling,
     box_sources, box_coupling, near_blocks, near_pairs, near_count,
 ):
-    smem = pl.BlockSpec(memory_space=pltpu.SMEM)
     hbm = pl.BlockSpec(memory_space=pl.ANY)
     products = jax.ShapeDtypeStruct((2, LEAVES, RHS, PANELS), BF16)
     values = pltpu.VMEM((GROUP, HALF, PANELS), BF16)
     coefs = pltpu.VMEM((NY, 2, RHS, 2 * RANK), BF16)
-    boxes = pltpu.VMEM((NX, NZ * NY, HALF, 2 * RANK), BF16)
+    boxes = pltpu.VMEM((BOXES + 1, HALF, 2 * RANK), BF16)
     part = pltpu.VMEM((2, NY, LEAVES * HALF, PANELS), BF16)
     got = pltpu.VMEM((2, NY - 1, LEAVES * HALF, PANELS), BF16)
     field = pltpu.VMEM((RHS, RANK), F32)
     both = pl.pallas_call(
         kernel,
         out_shape=products,
-        in_specs=[smem] * 4 + [hbm] * 7,
+        in_specs=[hbm] * 10,
         out_specs=hbm,
         scratch_shapes=[
             pltpu.VMEM((LEAVES, RANK, PANELS), BF16),
@@ -348,17 +379,23 @@
             field, field, field, field,
             pltpu.VMEM((1, FAR_BOX), jnp.int32),
             pltpu.SMEM((1, FAR_BOX), jnp.int32),
-            pltpu.SemaphoreType.DMA((9,)),
+            pltpu.SMEM((2, SLOTS), jnp.int32),
+            pltpu.SMEM((1,), jnp.int32),
+            pltpu.SMEM((LEAVES, FAR_LEAF), jnp.int32),
+            pltpu.SMEM((1, FAR_BOX), jnp.int32),
+            pltpu.SMEM((2, FAR_BOX), jnp.int32),
+            pltpu.VMEM((RANK, LEAVES * PANELS), BF16),
+            pltpu.SemaphoreType.DMA((13,)),
             pltpu.SemaphoreType.DMA((2, 2)),
-            pltpu.SemaphoreType.DMA((2, 14)),
-            pltpu.SemaphoreType.DMA((2, 14)),
+            pltpu.SemaphoreType.DMA((2, 15)),
+            pltpu.SemaphoreType.DMA((2, 15)),
         ],
         compiler_params=pltpu.CompilerParams(
             collective_id=0, has_side_effects=True, vmem_limit_bytes=63 << 20
         ),
         name="two_products",
     )(
-        near_pairs.T, near_count, leaf_sources, box_sources, box_sources,
+        near_pairs.T, near_count, leaf_sources, box_sources,
         panels, jnp.swapaxes(leaf_basis, 1, 2), transfer, leaf_coupling,
         box_coupling, near_blocks,
     )

time: 55.8 us -> 53.1 us (0.952)
  Pallas kernels: 52.9 us -> 50.2 us
    pallas_call x1, Pallas kernels: 52.9 us -> 50.2 us  [on_device(): pl.pallas_call(kernel, out_shape=products, in_specs=[hbm] * 10, out_specs...]
where the time goes in v3:
time: 53.1 us; the launch traced here: 52.9 us
  Pallas kernels  50.2 us (95%)
  local copies, waits for them, and re-layouts  1.4 us (3%)
  between operations  1.29 us (2%)
    pallas_call x1, Pallas kernels, on_device(): pl.pallas_call(kernel, out_shape=products, in_specs=[hbm] * 10, out_specs...  50.2 us
    squeeze x1, local copies, waits for them, and re-layouts, on_device(): return (both[0], both[1])  1.4 us

profile of v3, /device:TPU:1, one launch (start us, length us, event | category | flops | bytes accessed | tf_op | source)
XLA Modules:
  0.0 52.9 jit_solution(18030797350027281808)
XLA Ops:
  1.3 50.2 %two_products.1 = bf16[2,4,16,256]{3,2,1,0:T(8,128)(2,1)} custom-call(s32[2,16]{1,0:T(2,128)} %bitcast.7, s32[1]{0:T(128)S(6)} %copy.12.count_hbm, s32[4,8]{1,0:T(4,128)} %leaf_src_hbm.1, s32[1,32]{1,0:T(1,128)} %box_src_hbm.1, bf16[4,16,256]{2,1,0:T(8,128)(2,1)} %panels_hbm.1, bf16[4,64,256]{2,1,0:T(8,128)(2,1)} %bitcast.6, ...), custom_call_target="tpu_custom_call" | custom-call | tf_op jit(solution)/shard_map/two_products/pallas_call | solution.py:360
  51.5 1.4 %slice_bitcast_fusion = (bf16[4,16,256]{2,1,0:T(8,128)(2,1)}, bf16[4,16,256]{2,1,0:T(8,128)(2,1)}) fusion(bf16[2,4,16,256]{3,2,1,0:T(8,128)(2,1)} %two_products.1), kind=kLoop, calls=%fused_computation | loop fusion | bytes 131072 | tf_op jit(solution)/shard_map/squeeze | solution.py:402

commit v4 on v3

--- a/solution.py
+++ b/solution.py
@@ -5,7 +5,7 @@
 from jax.experimental.pallas import tpu as pltpu
 from jax.sharding import PartitionSpec as P
 
-MESH = pl.DeviceIdType.MESH
+MESH = pl.DeviceIdType.LOGICAL
 F32 = jnp.float32
 BF16 = jnp.bfloat16
 NY, NZ, NX = 8, 8, 4
@@ -55,7 +55,7 @@
     z = lax.div(clus, 2 * NX)
 
     def at(zz, xx, cc, yy):
-        return ((zz * NX + xx) * 2 + cc, yy)
+        return ((zz * NX + xx) * 2 + cc) * NY + yy
 
     def y_peer(d):
         return at(z, x, core, lax.rem(y + d, NY))
@@ -174,9 +174,16 @@
     def finish(p, k, whole):
         pltpu.make_async_copy(whole, whole, recv_sem.at[p, k]).wait()
 
-    V0, V1, C, YN, YF, Z1, Z2, Z3, Z4, X, K, R0, R1, W, S = range(15)
-    z_chunks = ((Z1, 1, 3), (Z2, 3, 5), (Z3, 5, 7), (Z4, 7, 8))
+    V0, V1, C, YN, YF, X, K, R0, R1, W, S, Z1, Z2 = range(13)
+    z_chunks = tuple((Z1 + i, i + 1, i + 2) for i in range(7))
     z_sem = {slot: k for k, a, b in z_chunks for slot in range(a, b)}
+
+    def store(p, h):
+        return pltpu.make_async_copy(
+            (vals10, vals11)[h].at[own] if p == 0 else last.at[h],
+            out_hbm.at[p, :, pl.ds(h * HALF, HALF)],
+            store_sem.at[p, h],
+        )
 
     for p in range(2):
         val, coef, box = (
@@ -218,6 +225,9 @@
         for d in FAR_FIRST:
             group.start(coef.at[y], coef.at[y], y_peer(d))
 
+        if p == 1:
+            for h in range(2):
+                store(0, h).start()
         if p == 0:
             prepare()
             for i in (5, 6, 7):
@@ -264,7 +274,7 @@
 
         send_x(0, 1)
         near_half(0)
-        for chunk in range(4):
+        for chunk in range(7):
             forward(chunk)
         near_half(1)
 
@@ -304,18 +314,18 @@
         give[...] = box_part(1)
         Sends(p, K, take).start(give, take, other)
         box_field = box_part(0)
-        finish(p, K, take)
-        box_field = (box_field + take[...]).astype(BF16)
-        from_box = dot(box_field, down[...])
-
-        result = []
+        totals = []
         for h in range(2):
             finish(p, (R0, R1)[h], got.at[h])
             near = part[h, y].astype(F32)
             for d in range(1, NY):
                 near = near + got[h, d - 1].astype(F32)
-            near = near + from_leaves[h * LEAVES * HALF : (h + 1) * LEAVES * HALF]
-            near = near + jnp.concatenate(
+            totals.append(near + from_leaves[h * LEAVES * HALF : (h + 1) * LEAVES * HALF])
+        finish(p, K, take)
+        box_field = (box_field + take[...]).astype(BF16)
+        from_box = dot(box_field, down[...])
+        for h in range(2):
+            near = totals[h] + jnp.concatenate(
                 [
                     from_box[h * HALF : (h + 1) * HALF, t * PANELS : (t + 1) * PANELS]
                     for t in range(LEAVES)
@@ -327,22 +337,14 @@
                 (vals10, vals11)[h][own] = near
             else:
                 last[h] = near
-        for h in range(2):
-            pltpu.make_async_copy(
-                (vals10, vals11)[h].at[own] if p == 0 else last.at[h],
-                out_hbm.at[p, :, pl.ds(h * HALF, HALF)],
-                store_sem.at[p, h],
-            ).start()
-
+
+    for h in range(2):
+        store(1, h).start()
     for whole, sem in pending:
         pltpu.make_async_copy(whole, whole, sem).wait()
     for p in range(2):
         for h in range(2):
-            pltpu.make_async_copy(
-                (vals10, vals11)[h].at[own] if p == 0 else last.at[h],
-                out_hbm.at[p, :, pl.ds(h * HALF, HALF)],
-                store_sem.at[p, h],
-            ).wait()
+            store(p, h).wait()
 
 
 def on_device(
@@ -387,8 +389,8 @@
             pltpu.VMEM((RANK, LEAVES * PANELS), BF16),
             pltpu.SemaphoreType.DMA((13,)),
             pltpu.SemaphoreType.DMA((2, 2)),
-            pltpu.SemaphoreType.DMA((2, 15)),
-            pltpu.SemaphoreType.DMA((2, 15)),
+            pltpu.SemaphoreType.DMA((2, 18)),
+            pltpu.SemaphoreType.DMA((2, 18)),
         ],
         compiler_params=pltpu.CompilerParams(
             collective_id=0, has_side_effects=True, vmem_limit_bytes=63 << 20

time: 53.1 us -> 52.4 us (0.987)
  Pallas kernels: 50.2 us -> 49.5 us
    pallas_call x1, Pallas kernels: 50.2 us -> 49.5 us  [on_device(): pl.pallas_call(kernel, out_shape=products, in_specs=[hbm] * 10, out_specs...]
where the time goes in v4:
time: 52.4 us; the launch traced here: 52.2 us
  Pallas kernels  49.5 us (94%)
  local copies, waits for them, and re-layouts  1.4 us (3%)
  between operations  1.29 us (2%)
    pallas_call x1, Pallas kernels, on_device(): pl.pallas_call(kernel, out_shape=products, in_specs=[hbm] * 10, out_specs...  49.5 us
    squeeze x1, local copies, waits for them, and re-layouts, on_device(): return (both[0], both[1])  1.4 us

profile of v4, /device:TPU:1, one launch (start us, length us, event | category | flops | bytes accessed | tf_op | source)
XLA Modules:
  0.0 52.2 jit_solution(14082480817311174698)
XLA Ops:
  1.3 49.5 %two_products.1 = bf16[2,4,16,256]{3,2,1,0:T(8,128)(2,1)} custom-call(s32[2,16]{1,0:T(2,128)} %bitcast.7, s32[1]{0:T(128)S(6)} %copy.12.count_hbm, s32[4,8]{1,0:T(4,128)} %leaf_src_hbm.1, s32[1,32]{1,0:T(1,128)} %box_src_hbm.1, bf16[4,16,256]{2,1,0:T(8,128)(2,1)} %panels_hbm.1, bf16[4,64,256]{2,1,0:T(8,128)(2,1)} %bitcast.6, ...), custom_call_target="tpu_custom_call" | custom-call | tf_op jit(solution)/shard_map/two_products/pallas_call | solution.py:362
  50.8 1.4 %slice_bitcast_fusion = (bf16[4,16,256]{2,1,0:T(8,128)(2,1)}, bf16[4,16,256]{2,1,0:T(8,128)(2,1)}) fusion(bf16[2,4,16,256]{3,2,1,0:T(8,128)(2,1)} %two_products.1), kind=kLoop, calls=%fused_computation | loop fusion | bytes 131072 | tf_op jit(solution)/shard_map/squeeze | solution.py:404
